TPU v7x, 256 devices: a whole 4x4x8 slice. The times are simulated.
256 devices in a mesh: dp: 32 (over x_lo, z, core), expert: 8 (over x_hi, y).
Axes of the slice: x: 4 (x_hi: 2, x_lo: 2; x = x_hi * 2 + x_lo), y: 4, z: 8, core: 2. Of those that a mesh axis runs over, the one named last changes fastest.
Arguments:
- tokens: bfloat16 [49152, 4096], P(('dp', 'expert')), may hold values from -24 to 24
- routes: int32 [49152, 2], P(('dp', 'expert')), may hold values from 0 to 7, all different within a row; in each aligned block of 192 rows (0 to 191, 192 to 383, ...) at most 64 rows name the same one
- positives: int32 [512], P(('dp', 'expert')), may hold values from 0 to 511, each once
- expert_out: bfloat16 [32, 8, 8, 64, 4096], P('dp', 'expert'), may hold values from -6 to 6
- router: bfloat16 [4096, 8], replicated, may hold values from -0.09375 to 0.09375
- norm_gain: float32 [4096], replicated, may hold values from 0.25 to 1.75
- loss_scale: float32 [], replicated, may hold values from 8192 to 65536
Outputs:
- token_grad: bfloat16 [49152, 4096], P(('dp', 'expert'))
- expert_grad: bfloat16 [32, 8, 8, 64, 4096], P('dp', 'expert')
- router_grad: float32 [4096, 8], replicated
- loss: float32 [], replicated
Inputs may be any that keep to these rules, and one draw needn't show every extreme that they name: `routes`: each row names 2 different experts; among the rows of one device no expert is named by more than 64 rows, a bound that some block reaches. `positives`: A permutation of the records.
All inputs are finite; a program needn't handle non-finite values.
Results may differ from a plain program's by a relative error of at most 0.0061.
Values may be sent and summed in bfloat16 or wider, within the bound.
No kernel may reach another device: no remote copies, remote signals or barrier semaphores. Data moves between devices by JAX's collectives and lax.ppermute only.
A program may use at most 128 MiB of HBM per device.

v0:
```python
import math
import jax
import jax.numpy as jnp
from jax import lax
from jax.sharding import PartitionSpec as P

PAIR_DEV = 2
SEQ = 48
norm_eps = 1e-05


def slot_where(routes, experts, capacity):
    hit_table = (routes[:, :, None] == jnp.arange(experts, dtype=jnp.int32)[None, None, :]).astype(
        jnp.int32
    )
    flat_hits = hit_table.reshape(-1, experts)
    before = jnp.cumsum(flat_hits, axis=0) - flat_hits
    slot_rank = jnp.sum(before * flat_hits, axis=1).reshape(routes.shape)
    return routes * capacity + slot_rank


def forward_rows(tokens, routes, received, router, norm_gain):
    experts = received.shape[0]
    capacity = received.shape[1]
    hidden_width = received.shape[2]
    logits = jnp.dot(tokens, router, preferred_element_type=jnp.float32)
    one_hot = (routes[:, :, None] == jnp.arange(experts, dtype=jnp.int32)[None, None, :]).astype(
        jnp.float32
    )
    chosen = jnp.sum(one_hot * logits[:, None, :], axis=2)
    gate_mix = jax.nn.softmax(chosen, axis=1)
    slot_rows = slot_where(routes, experts, capacity)
    fetched = received.reshape(experts * capacity, hidden_width)[slot_rows]
    summed_rows = (
        tokens.astype(jnp.float32)
        + gate_mix[:, 0:1] * fetched[:, 0].astype(jnp.float32)
        + gate_mix[:, 1:2] * fetched[:, 1].astype(jnp.float32)
    )
    inverse = lax.rsqrt(jnp.mean(summed_rows * summed_rows, axis=1, keepdims=True) + norm_eps)
    normed = summed_rows * inverse * norm_gain
    pooled = jnp.mean(normed.reshape(-1, SEQ, hidden_width), axis=1).astype(jnp.bfloat16)
    return (pooled, (gate_mix, one_hot, slot_rows, fetched, summed_rows, inverse))


def backward_rows(tokens, router, norm_gain, saved, grad_pool, experts, capacity):
    gate_mix, one_hot, slot_rows, fetched, summed_rows, inverse = saved
    hidden_width = tokens.shape[1]
    grad_rows = jnp.broadcast_to(
        grad_pool[:, None, :] / SEQ, (grad_pool.shape[0], SEQ, hidden_width)
    ).reshape(-1, hidden_width)
    weighted = grad_rows * norm_gain
    grad_summed = inverse * weighted - summed_rows * inverse**3 * jnp.mean(
        weighted * summed_rows, axis=1, keepdims=True
    )
    grad_gate = jnp.sum(grad_summed[:, None, :] * fetched.astype(jnp.float32), axis=2)
    grad_chosen = gate_mix * (grad_gate - jnp.sum(gate_mix * grad_gate, axis=1, keepdims=True))
    grad_logits = jnp.sum(one_hot * grad_chosen[:, :, None], axis=1).astype(jnp.bfloat16)
    router_part = lax.dot_general(
        tokens, grad_logits, (((0,), (0,)), ((), ())), preferred_element_type=jnp.float32
    )
    through_router = lax.dot_general(
        grad_logits, router, (((1,), (1,)), ((), ())), preferred_element_type=jnp.float32
    )
    token_grad = (grad_summed + through_router).astype(jnp.bfloat16)
    outgoing = (
        (gate_mix[:, :, None] * grad_summed[:, None, :])
        .astype(jnp.bfloat16)
        .reshape(-1, hidden_width)
    )
    sendback = (
        jnp.zeros((experts * capacity, hidden_width), jnp.bfloat16)
        .at[slot_rows.reshape(-1)]
        .set(outgoing)
    )
    return (token_grad, sendback.reshape(experts, capacity, hidden_width), router_part)


def score_rows(queries, records_all, positives, loss_scale, pair_total, score_scale):
    scores = (
        lax.dot_general(
            queries, records_all, (((1,), (1,)), ((), ())), preferred_element_type=jnp.float32
        )
        * score_scale
    )
    highest = jnp.max(scores, axis=1, keepdims=True)
    log_total = highest[:, 0] + jnp.log(jnp.sum(jnp.exp(scores - highest), axis=1))
    is_positive = jnp.arange(pair_total, dtype=jnp.int32)[None, :] == positives[:, None]
    positive_score = jnp.sum(jnp.where(is_positive, scores, jnp.zeros_like(scores)), axis=1)
    row_loss = log_total - positive_score
    softmax_rows = jnp.exp(scores - log_total[:, None])
    score_grad = (
        (softmax_rows - is_positive.astype(jnp.float32)) * (loss_scale / pair_total)
    ).astype(jnp.bfloat16)
    return (row_loss, score_grad)


def shards(tokens, routes, positives, expert_out, router, norm_gain, loss_scale):
    experts = expert_out.shape[2]
    capacity = expert_out.shape[3]
    hidden_width = expert_out.shape[4]
    received = lax.all_to_all(
        expert_out.reshape(experts, capacity, hidden_width),
        "expert",
        split_axis=0,
        concat_axis=0,
        tiled=True,
    )
    pooled, saved = forward_rows(tokens, routes, received, router, norm_gain)
    queries = pooled[:PAIR_DEV]
    records = pooled[PAIR_DEV:]
    loop_size = lax.axis_size("dp")
    column_size = lax.axis_size("expert")
    device_count = loop_size * column_size
    pair_total = PAIR_DEV * device_count
    score_scale = 4.0 / math.sqrt(hidden_width)
    records_all = lax.all_gather(records, ("dp", "expert"), axis=0, tiled=True)
    row_loss, score_grad = score_rows(
        queries, records_all, positives, loss_scale, pair_total, score_scale
    )
    loss_local = jnp.sum(row_loss)
    grad_queries = (
        jnp.dot(score_grad, records_all, preferred_element_type=jnp.float32) * score_scale
    )
    grad_records = lax.psum_scatter(
        lax.dot_general(
            score_grad, queries, (((0,), (0,)), ((), ())), preferred_element_type=jnp.float32
        )
        * score_scale,
        ("dp", "expert"),
        scatter_dimension=0,
        tiled=True,
    )
    grad_pool = jnp.concatenate([grad_queries, grad_records], axis=0)
    token_grad, sendback, router_part = backward_rows(
        tokens, router, norm_gain, saved, grad_pool, experts, capacity
    )
    returned = lax.all_to_all(sendback, "expert", split_axis=0, concat_axis=0, tiled=True)
    router_grad, loss_total = lax.psum((router_part, loss_local), ("dp", "expert"))
    expert_grad = returned.reshape(1, 1, experts, capacity, hidden_width)
    return (token_grad, expert_grad, router_grad, loss_total / pair_total)


def solution(mesh):
    placed = (
        P(("dp", "expert"), None),
        P(("dp", "expert"), None),
        P(("dp", "expert")),
        P("dp", "expert", None, None, None),
        P(),
        P(),
        P(),
    )
    return jax.shard_map(
        shards,
        mesh=mesh,
        in_specs=placed,
        out_specs=(P(("dp", "expert"), None), P("dp", "expert", None, None, None), P(), P()),
        check_vma=False,
    )
```

profile of v0, /device:TPU:8, one launch (start us, length us, event | category | flops | bytes accessed | tf_op | source)
XLA Modules:
  0.0 1506.5 jit_solution(1943185011051784695)
XLA Ops:
  7.2 7.5 all-to-all-start
  17.5 45.7 %all-to-all-done = bf16[8,64,4096]{2,1,0:T(8,128)(2,1)} async-done(((bf16[8,64,4096]{2,1,0:T(8,128)(2,1)}), bf16[8,64,4096]{2,1,0:T(8,128)(2,1)}, u32[]{:S(2)}, u32[]{:S(2)}) %all-to-all-start) | async-done | bytes 4194336 | tf_op jit(solution)/shard_map/all_to_all | solution.py:101
  63.2 11.0 gather_fusion
  74.2 4.6 reshape.220
  78.8 7.0 fusion.17
  85.8 4.0 multiply_reduce_fusion.2
  89.9 2.4 multiply_multiply_fusion
  92.5 2.2 reduce_sum.112
  96.2 680.8 %all-gather.3.cloned.1.call-done = bf16[256,2,4096]{2,1,0:T(2,128)(2,1)} async-done(((bf16[1,2,4096]{2,1,0:T(2,128)(2,1)}), bf16[256,2,4096]{2,1,0:T(2,128)(2,1)}) %all-gather.3.cloned.1.call-update) | async-done | bytes 4194320 | tf_op jit(solution)/shard_map/all_gather | solution.py:116
  777.0 7.2 reshape.238
  784.2 3.5 fusion.19
  788.5 4.6 convolution_multiply_fusion
  793.7 2.9 convolution_multiply_fusion.1
  796.6 301.1 %all-reduce.6.cloned.1.call-done = f32[512,4096]{1,0:T(8,128)} async-done(((f32[512,4096]{1,0:T(8,128)}), f32[512,4096]{1,0:T(8,128)}) %all-reduce.6.cloned.1.call-update) | async-done | bytes 8388624
  1102.5 5.3 mul.182
  1107.8 8.4 mul.189
  1116.2 9.7 scatter_custom_fusion
  1125.9 6.8 all-to-all-start.1
  1132.6 112.4 %psum.15 = f32[]{:T(128)} all-reduce(f32[]{:T(128)} %get-tuple-element.6), channel_id=1, replica_groups=mesh['dp'=32,'expert'=8] {'dp','expert'}, use_global_device_ids=true, to_apply=%region_19.20 | all-reduce | flops 1 | bytes 8 | tf_op jit(solution)/shard_map/psum | solution.py:138
  1245.7 5.7 multiply_reduce_fusion
  1251.5 2.4 convolution_bitcast_fusion
  1254.0 3.6 fusion
  1257.6 235.8 %all-reduce.4.cloned.1.call-done = f32[4096,8]{0,1:T(8,128)} async-done(((f32[4096,8]{0,1:T(8,128)}), f32[4096,8]{0,1:T(8,128)}) %all-reduce.4.cloned.1.call-update) | async-done | bytes 131088 | tf_op jit(solution)/shard_map/psum | solution.py:138
  1493.4 4.7 copy.69
  (68 shorter events, 10.8 us)
Async XLA Ops:
  7.2 9.7 copy-start
  7.2 7.5 copy-start.8
  7.2 9.7 copy-start.4
  7.2 56.0 %all-to-all-start = ((bf16[8,64,4096]{2,1,0:T(8,128)(2,1)}), bf16[8,64,4096]{2,1,0:T(8,128)(2,1)}, u32[]{:S(2)}, u32[]{:S(2)}) async-start(bf16[8,64,4096]{2,1,0:T(8,128)(2,1)} %bitcast.46), calls=%async_computation | async-start | bytes 8388608 | tf_op jit(solution)/shard_map/all_to_all | solution.py:101
  14.7 762.3 %all-gather.3.cloned.1.call-start = ((), (), s32[]{:S(2)}) async-start(), calls=%async_computation.3 | async-start | bytes 4210688 | tf_op jit(solution)/shard_map/all_gather | solution.py:116
  78.8 7.0 copy-start.5
  85.8 4.1 copy-start.6
  89.8 2.6 copy-start.2
  95.3 1002.4 %all-reduce.6.cloned.1.call-start = ((), (), s32[]{:S(2)}) async-start(), calls=%async_computation.4 | async-start | bytes 16777216
  784.2 3.5 copy-start.9
  1097.7 2.0 copy-start.3
  1100.8 1.7 copy-start.1
  1125.9 131.7 %all-to-all-start.1 = ((bf16[8,64,4096]{2,1,0:T(8,128)(2,1)}), bf16[8,64,4096]{2,1,0:T(8,128)(2,1)}, u32[]{:S(2)}, u32[]{:S(2)}) async-start(bf16[8,64,4096]{2,1,0:T(8,128)(2,1)} %bitcast.44), calls=%async_computation.1 | async-start | bytes 8388608 | tf_op jit(solution)/shard_map/all_to_all | solution.py:137
  1132.6 360.8 %all-reduce.4.cloned.1.call-start = ((), (), s32[]{:S(2)}) async-start(), calls=%async_computation.2 | async-start | bytes 262144 | tf_op jit(solution)/shard_map/psum | solution.py:138
  1493.4 4.7 copy-start.7
Sparse Core Ops, SparseCore 0:
  95.4 681.5 all-gather.2
  793.3 304.4 all-reduce.5
  1254.1 239.3 all-reduce.3
where the time goes:
time: 1510 us
  waiting for transfers between devices  1260 us (83%)
  blocking collectives  112 us (7%)
  local copies, waits for them, and re-layouts  54.7 us (4%)
  other arithmetic  27.5 us (2%)
  matrix products  17.5 us (1%)
  between operations  16.5 us (1%)
    all_gather x1, waiting for transfers between devices, shards(): records_all = lax.all_gather(records, ('dp', 'expert'), axis=0, tiled=True)  681 us
    unnamed x4, waiting for transfers between devices  301 us
    psum x1, waiting for transfers between devices, shards(): lax.psum((router_part, loss_local), ('dp', 'expert'))  236 us
    psum x1, blocking collectives, shards(): lax.psum((router_part, loss_local), ('dp', 'expert'))  112 us
    all_to_all x1, waiting for transfers between devices, shards(): lax.all_to_all(expert_out.reshape(experts, capacity, hidden_width), 'expe...  45.7 us
  transfers between devices with their start and end apart: 5, of which 4 were waited for; matrix products, arithmetic and copies ran while one was open for 1% of the time, Pallas kernels for 0%

commit v1 on v0

--- a/solution.py
+++ b/solution.py
@@ -113,7 +113,16 @@
     device_count = loop_size * column_size
     pair_total = PAIR_DEV * device_count
     score_scale = 4.0 / math.sqrt(hidden_width)
-    records_all = lax.all_gather(records, ("dp", "expert"), axis=0, tiled=True)
+    detail_forms = lambda here_x: jnp.concatenate(
+        lax.all_to_all(
+            jnp.stack([here_x for _ in range(lax.psum(1, ("dp", "expert")))], axis=0),
+            ("dp", "expert"),
+            0,
+            0,
+        ),
+        0,
+    )
+    records_all = detail_forms(records)
     row_loss, score_grad = score_rows(
         queries, records_all, positives, loss_scale, pair_total, score_scale
     )

time: 1510 us -> 912 us (0.60)
  waiting for transfers between devices: 1260 us -> 648 us
    all_gather x1 -> x0, waiting for transfers between devices: 681 us -> none  [shards(): records_all = lax.all_gather(records, ('dp', 'expert'), axis=0, tiled=True)]
    all_to_all x0 -> x1, waiting for transfers between devices: none -> 94.9 us  [shards(): lax.all_to_all(jnp.stack([here_x for _ in range(lax.psum(1, ('dp', 'exper...]
    unnamed x4 -> x3, waiting for transfers between devices: 301 us -> 272 us
  transfers between devices with their start and end apart: 5 -> 5, of which waited for: 4 -> 4; matrix products, arithmetic and copies ran while one was open for 1% -> 2% of each run, Pallas kernels for 0% -> 0%
where the time goes in v1:
time: 912 us; the launch traced here: 910 us
  waiting for transfers between devices  648 us (71%)
  blocking collectives  112 us (12%)
  local copies, waits for them, and re-layouts  60.5 us (7%)
  starting transfers between devices  27.8 us (3%)
  other arithmetic  27.5 us (3%)
  matrix products  17.5 us (2%)
  between operations  16.8 us (2%)
    unnamed x3, waiting for transfers between devices  272 us
    psum x1, waiting for transfers between devices, shards(): lax.psum((router_part, loss_local), ('dp', 'expert'))  236 us
    psum x1, blocking collectives, shards(): lax.psum((router_part, loss_local), ('dp', 'expert'))  112 us
    all_to_all x1, waiting for transfers between devices, shards(): lax.all_to_all(jnp.stack([here_x for _ in range(lax.psum(1, ('dp', 'exper...  94.9 us
    all_to_all x1, waiting for transfers between devices, shards(): lax.all_to_all(expert_out.reshape(experts, capacity, hidden_width), 'expe...  45.7 us
  transfers between devices with their start and end apart: 5, of which 4 were waited for; matrix products, arithmetic and copies ran while one was open for 2% of the time, Pallas kernels for 0%

profile of v1, /device:TPU:8, one launch (start us, length us, event | category | flops | bytes accessed | tf_op | source)
XLA Modules:
  0.0 910.4 jit_solution(16754102881701877243)
XLA Ops:
  7.2 7.5 all-to-all-start
  17.5 45.7 %all-to-all-done = bf16[8,64,4096]{2,1,0:T(8,128)(2,1)} async-done(((bf16[8,64,4096]{2,1,0:T(8,128)(2,1)}), bf16[8,64,4096]{2,1,0:T(8,128)(2,1)}, u32[]{:S(2)}, u32[]{:S(2)}) %all-to-all-start) | async-done | bytes 4194336 | tf_op jit(solution)/shard_map/all_to_all | solution.py:101
  63.2 11.0 %gather_fusion = bf16[384,4096]{1,0:T(8,128)(2,1)} fusion(bf16[512,4096]{1,0:T(8,128)(2,1)} %bitcast.2, s32[1024]{0:T(1024)S(1)} %pad_clamp_fusion), kind=kCustom, calls=%fused_computation | custom fusion | bytes 6292992 | tf_op jit(solution)/shard_map/gather | solution.py:33
  74.2 4.6 reshape.226
  78.8 7.2 fusion.17
  86.0 4.0 multiply_reduce_fusion.2
  90.0 2.4 multiply_multiply_fusion
  94.9 6.3 stack.2
  101.1 13.5 %all-to-all-start.1 = ((bf16[256,2,4096]{2,1,0:T(2,128)(2,1)}), bf16[256,2,4096]{2,1,0:T(2,128)(2,1)}, u32[]{:S(2)}, u32[]{:S(2)}) async-start(bf16[256,2,4096]{2,1,0:T(2,128)(2,1)} %stack.2), calls=%async_computation.1 | async-start | bytes 8388608 | tf_op jit(solution)/shard_map/all_to_all | solution.py:117
  115.4 94.9 %all-to-all-done.1 = bf16[256,2,4096]{2,1,0:T(2,128)(2,1)} async-done(((bf16[256,2,4096]{2,1,0:T(2,128)(2,1)}), bf16[256,2,4096]{2,1,0:T(2,128)(2,1)}, u32[]{:S(2)}, u32[]{:S(2)}) %all-to-all-start.1) | async-done | bytes 4194336 | tf_op jit(solution)/shard_map/all_to_all | solution.py:117
  210.3 7.2 reshape.218
  217.4 3.5 fusion.19
  221.8 4.6 convolution_multiply_fusion
  227.0 2.9 convolution_multiply_fusion.1
  229.9 271.5 %all-reduce.6.cloned.1.call-done = f32[512,4096]{1,0:T(8,128)} async-done(((f32[512,4096]{1,0:T(8,128)}), f32[512,4096]{1,0:T(8,128)}) %all-reduce.6.cloned.1.call-update) | async-done | bytes 8388624
  506.1 5.3 mul.182
  511.4 8.4 mul.189
  519.9 9.7 %scatter_custom_fusion = bf16[512,4096]{1,0:T(8,128)(2,1)} fusion(s32[384]{0:T(512)S(1)} %fusion.13, f32[384,4096]{1,0:T(8,128)} %mul.189, f32[384]{0:T(512)S(1)} %div.48, bf16[]{:T(256)} %constant.41.clone.1), kind=kCustom, calls=%fused_computation.9 | custom fusion | flops 3145728 | bytes 10487810 | tf_op jit(solution)/shard_map/scatter | solution.py:73
  529.5 6.8 all-to-all-start.2
  536.3 112.4 %psum.15 = f32[]{:T(128)} all-reduce(f32[]{:T(128)} %get-tuple-element.6), channel_id=1, replica_groups=mesh['dp'=32,'expert'=8] {'dp','expert'}, use_global_device_ids=true, to_apply=%region_19.20 | all-reduce | flops 1 | bytes 8 | tf_op jit(solution)/shard_map/psum | solution.py:147
  649.3 5.7 multiply_reduce_fusion
  657.6 3.6 fusion
  661.3 235.8 %all-reduce.4.cloned.1.call-done = f32[4096,8]{0,1:T(8,128)} async-done(((f32[4096,8]{0,1:T(8,128)}), f32[4096,8]{0,1:T(8,128)}) %all-reduce.4.cloned.1.call-update) | async-done | bytes 131088 | tf_op jit(solution)/shard_map/psum | solution.py:147
  897.1 4.7 copy.69
  (68 shorter events, 14.5 us)
Async XLA Ops:
  7.2 9.7 %copy-start = (bf16[4096,8]{0,1:T(8,128)(2,1)S(1)}, bf16[4096,8]{0,1:T(8,128)(2,1)}, u32[]{:S(2)}) copy-start(bf16[4096,8]{0,1:T(8,128)(2,1)} %param.11) | copy-start | bytes 196612
  7.2 7.5 copy-start.8
  7.2 9.7 %copy-start.4 = (bf16[192,4096]{1,0:T(8,128)(2,1)S(1)}, bf16[192,4096]{1,0:T(8,128)(2,1)}, u32[]{:S(2)}) copy-start(bf16[192,4096]{1,0:T(8,128)(2,1)} %param.7) | copy-start | bytes 4718596
  7.2 56.0 %all-to-all-start = ((bf16[8,64,4096]{2,1,0:T(8,128)(2,1)}), bf16[8,64,4096]{2,1,0:T(8,128)(2,1)}, u32[]{:S(2)}, u32[]{:S(2)}) async-start(bf16[8,64,4096]{2,1,0:T(8,128)(2,1)} %bitcast.44), calls=%async_computation | async-start | bytes 8388608 | tf_op jit(solution)/shard_map/all_to_all | solution.py:101
  78.8 7.2 copy-start.5
  86.0 4.1 copy-start.6
  90.0 2.6 copy-start.2
  101.1 109.1 %all-to-all-start.1 = ((bf16[256,2,4096]{2,1,0:T(2,128)(2,1)}), bf16[256,2,4096]{2,1,0:T(2,128)(2,1)}, u32[]{:S(2)}, u32[]{:S(2)}) async-start(bf16[256,2,4096]{2,1,0:T(2,128)(2,1)} %stack.2), calls=%async_computation.1 | async-start | bytes 8388608 | tf_op jit(solution)/shard_map/all_to_all | solution.py:117
  114.7 386.7 %all-reduce.6.cloned.1.call-start = ((), (), s32[]{:S(2)}) async-start(), calls=%async_computation.4 | async-start | bytes 16777216
  217.4 3.5 copy-start.9
  501.4 2.0 copy-start.3
  504.5 1.7 copy-start.1
  529.5 131.7 %all-to-all-start.2 = ((bf16[8,64,4096]{2,1,0:T(8,128)(2,1)}), bf16[8,64,4096]{2,1,0:T(8,128)(2,1)}, u32[]{:S(2)}, u32[]{:S(2)}) async-start(bf16[8,64,4096]{2,1,0:T(8,128)(2,1)} %bitcast.42), calls=%async_computation.2 | async-start | bytes 8388608 | tf_op jit(solution)/shard_map/all_to_all | solution.py:146
  536.3 360.8 %all-reduce.4.cloned.1.call-start = ((), (), s32[]{:S(2)}) async-start(), calls=%async_computation.3 | async-start | bytes 262144 | tf_op jit(solution)/shard_map/psum | solution.py:147
  897.1 4.7 copy-start.7
Sparse Core Ops, SparseCore 0:
  226.5 274.8 all-reduce.5
  657.7 239.3 all-reduce.3
